TPU v7x, 32 devices: a whole 2x2x4 slice. The times are simulated.
32 devices in a mesh: row: 4 (over z), col: 8 (over y, x, core).
Axes of the slice: x: 2, y: 2, z: 4, core: 2. Of those that a mesh axis runs over, the one named last changes fastest.
Arguments:
- gaussian_sketch: bfloat16 [16384, 256], P(('col', 'row')), may hold values from -6 to 6
- block_values: bfloat16 [8192, 128, 128], P(('row', 'col')), may hold values from -6 to 6
- block_rows: int32 [8192], P(('row', 'col')), may hold values from 0 to 127, as said below
- block_columns: int32 [8192], P(('row', 'col')), may hold values from 0 to 127, as said below
Outputs:
- range_basis: float32 [16384, 256], P(('row', 'col'))
- upper_factor: float32 [256, 256], replicated
Inputs may be any that keep to these rules, and one draw needn't show every extreme that they name: `block_rows`: entry k * 256 + m, k = i * 8 + j, names a block row in [i * 32, (i + 1) * 32); no (row, column) pair is named twice. `block_columns`: entry k * 256 + m, k = i * 8 + j, names a block column in [j * 16, (j + 1) * 16).
All inputs are finite; a program needn't handle non-finite values.
Results may differ from a plain program's by a relative error of at most 0.0003.
Values may be sent and summed in bfloat16 or wider, within the bound.
No kernel may reach another device: no remote copies, remote signals or barrier semaphores. Data moves between devices by JAX's collectives and lax.ppermute only.
A program may use at most 128 MiB of HBM per device.

v0:
```python
import math
import jax
import jax.numpy as jnp
from jax import lax
from jax.sharding import PartitionSpec as P

PANEL = 128


def upper_parts(gram):
    lower_factor = jnp.linalg.cholesky(gram)
    identity = jnp.eye(gram.shape[0], dtype=gram.dtype)
    inverse = lax.linalg.triangular_solve(lower_factor, identity, left_side=True, lower=True)
    return (lower_factor.T, inverse.T)


def tile_product(sketch_blocks, block_values, local_rows, local_cols, tile_rows):
    group_size = math.gcd(block_values.shape[0], 64)
    col_width = sketch_blocks.shape[2]

    def advance(counter, summed):
        offset = (counter * group_size).astype(jnp.int32)
        values = lax.dynamic_slice_in_dim(block_values, offset, group_size, 0)
        row_ids = lax.dynamic_slice_in_dim(local_rows, offset, group_size, 0)
        col_ids = lax.dynamic_slice_in_dim(local_cols, offset, group_size, 0)
        picked = jnp.take(sketch_blocks, col_ids, axis=0)
        product = jnp.einsum("gab,gbs->gas", values, picked, preferred_element_type=jnp.float32)
        return summed.at[row_ids].add(product)

    initial = jnp.zeros((tile_rows, block_values.shape[1], col_width), jnp.float32)
    summed = lax.fori_loop(0, block_values.shape[0] // group_size, advance, initial)
    return summed.reshape(tile_rows * block_values.shape[1], col_width)


def on_device(gaussian_sketch, block_values, block_rows, block_columns):
    high = lax.Precision.HIGHEST
    size_row = lax.axis_size("row")
    size_col = lax.axis_size("col")
    shard_rows = gaussian_sketch.shape[0]
    block_size = block_values.shape[1]
    grid_rows = shard_rows * size_col // block_size
    grid_cols = shard_rows * size_row // block_size
    local_rows = block_rows - lax.axis_index("row") * grid_rows
    local_cols = block_columns - lax.axis_index("col") * grid_cols
    gathered = lax.all_gather(gaussian_sketch, "row", axis=0, tiled=True)
    sketch_blocks = gathered.reshape(grid_cols, block_size, gathered.shape[1])
    partial_value = tile_product(sketch_blocks, block_values, local_rows, local_cols, grid_rows)
    sketched = lax.psum_scatter(partial_value, "col", scatter_dimension=0, tiled=True)
    first_part = sketched[:, :PANEL]
    second_part = sketched[:, PANEL:]
    order_total = shard_rows * size_row * size_col
    gram_one = (
        lax.psum(jnp.dot(first_part.T, first_part, precision=high), ("row", "col")) / order_total
    )
    upper_one, inverse_one = upper_parts(gram_one)
    basis_one = jnp.dot(first_part, inverse_one, precision=high)
    coupling = (
        lax.psum(jnp.dot(basis_one.T, second_part, precision=high), ("row", "col")) / order_total
    )
    remainder = second_part - jnp.dot(basis_one, coupling, precision=high)
    gram_two = (
        lax.psum(jnp.dot(remainder.T, remainder, precision=high), ("row", "col")) / order_total
    )
    upper_two, inverse_two = upper_parts(gram_two)
    basis_two = jnp.dot(remainder, inverse_two, precision=high)
    range_basis = jnp.concatenate([basis_one, basis_two], axis=1)
    top_rows = jnp.concatenate([upper_one, coupling], axis=1)
    bottom_rows = jnp.concatenate([jnp.zeros_like(upper_two), upper_two], axis=1)
    upper_factor = jnp.concatenate([top_rows, bottom_rows], axis=0)
    return (range_basis, upper_factor)


def solution(mesh):
    return jax.shard_map(
        on_device,
        mesh=mesh,
        in_specs=(
            P(("col", "row"), None),
            P(("row", "col"), None, None),
            P(("row", "col")),
            P(("row", "col")),
        ),
        out_specs=(P(("row", "col"), None), P()),
        check_vma=False,
    )
```

profile of v0, /device:TPU:1, one launch (start us, length us, event | category | flops | bytes accessed | tf_op | source)
XLA Modules:
  0.0 643.8 jit_solution(3256187784970648376)
XLA Ops:
  7.2 0.0 all-gather.2.cloned.1.call-start
  7.2 0.7 all-gather.2.cloned.1.call-update
  7.9 0.0 reduce-scatter.2.cloned.1.call-start
  8.0 0.7 broadcast_subtract_fusion
  8.7 30.8 %all-gather.2.cloned.1.call-done = bf16[2048,256]{1,0:T(8,128)(2,1)} async-done(((bf16[512,256]{1,0:T(8,128)(2,1)}), bf16[2048,256]{1,0:T(8,128)(2,1)}) %all-gather.2.cloned.1.call-update) | async-done | bytes 1048592 | tf_op jit(solution)/shard_map/all_gather | solution.py:45
  39.5 2.5 broadcast_in_dim.36
  41.9 0.0 copy-done
  41.9 118.3 %while.13 = (s32[]{:T(128)}, f32[32,128,256]{2,1,0:T(8,128)}, s32[256]{0:T(256)S(1)}, bf16[256,128,128]{2,1,0:T(8,128)(2,1)}, s32[256]{0:T(256)S(1)}, /*index=5*...) while((s32[]{:T(128)}, f32[32,128,256]{2,1,0:T(8,128)}, s32[256]{0:T(256)S(1)}, ...), condition=%wide.region_2.3_spmd, body=%wide.region_0.2_spmd.sunk | while | flops 541066816 | bytes 48240672 | solution.py:31
  41.9 0.1 compare_and_fusion.2
  42.0 2.8 gather_fusion
  44.8 7.4 %fusion.38 = f32[64,128,256]{2,1,0:T(8,128)} fusion(bf16[64,128,256]{2,1,0:T(8,128)(2,1)} %gather_fusion, pred[64]{0:T(512)(128)(4,1)S(1)} %get-tuple-element.176, bf16[256,128,128]{2,1,0:T(8,128)(2,1)} %get-tuple-element.200, s32[]{:T(128)S(6)} %select_n.59), kind=kOutput, calls=%fused_computation.2.clone.1 | convolution fusion | flops 538968064 | bytes 14680132 | tf_op jit(solution)/shard_map/while/body/eval_jaxpr/gab,gbs->gas/dot_general | solution.py:27
  52.2 0.1 compare_select_fusion.4
  52.3 19.2 %scatter_fusion = f32[32,128,256]{2,1,0:T(8,128)} fusion(f32[32,128,256]{2,1,0:T(8,128)} %get-tuple-element.188, s32[64]{0:T(128)S(1)} %compare_select_fusion.4, f32[64,128,256]{2,1,0:T(8,128)} %fusion.38), kind=kCustom, calls=%fused_computation.1.clone.1 | custom fusion | flops 2097152 | bytes 25166080 | tf_op jit(solution)/shard_map/while/body/eval_jaxpr/scatter-add | solution.py:28
  71.4 0.1 compare_and_fusion.2
  71.5 2.8 gather_fusion
  74.3 7.4 %fusion.38 = f32[64,128,256]{2,1,0:T(8,128)} fusion(bf16[64,128,256]{2,1,0:T(8,128)(2,1)} %gather_fusion, pred[64]{0:T(512)(128)(4,1)S(1)} %get-tuple-element.176, bf16[256,128,128]{2,1,0:T(8,128)(2,1)} %get-tuple-element.200, s32[]{:T(128)S(6)} %select_n.59), kind=kOutput, calls=%fused_computation.2.clone.1 | convolution fusion | flops 538968064 | bytes 14680132 | tf_op jit(solution)/shard_map/while/body/eval_jaxpr/gab,gbs->gas/dot_general | solution.py:27
  81.7 0.1 compare_select_fusion.4
  81.7 19.1 %scatter_fusion = f32[32,128,256]{2,1,0:T(8,128)} fusion(f32[32,128,256]{2,1,0:T(8,128)} %get-tuple-element.188, s32[64]{0:T(128)S(1)} %compare_select_fusion.4, f32[64,128,256]{2,1,0:T(8,128)} %fusion.38), kind=kCustom, calls=%fused_computation.1.clone.1 | custom fusion | flops 2097152 | bytes 25166080 | tf_op jit(solution)/shard_map/while/body/eval_jaxpr/scatter-add | solution.py:28
  100.9 0.1 compare_and_fusion.2
  101.0 2.8 gather_fusion
  103.7 7.4 %fusion.38 = f32[64,128,256]{2,1,0:T(8,128)} fusion(bf16[64,128,256]{2,1,0:T(8,128)(2,1)} %gather_fusion, pred[64]{0:T(512)(128)(4,1)S(1)} %get-tuple-element.176, bf16[256,128,128]{2,1,0:T(8,128)(2,1)} %get-tuple-element.200, s32[]{:T(128)S(6)} %select_n.59), kind=kOutput, calls=%fused_computation.2.clone.1 | convolution fusion | flops 538968064 | bytes 14680132 | tf_op jit(solution)/shard_map/while/body/eval_jaxpr/gab,gbs->gas/dot_general | solution.py:27
  111.1 0.1 compare_select_fusion.4
  111.2 19.6 %scatter_fusion = f32[32,128,256]{2,1,0:T(8,128)} fusion(f32[32,128,256]{2,1,0:T(8,128)} %get-tuple-element.188, s32[64]{0:T(128)S(1)} %compare_select_fusion.4, f32[64,128,256]{2,1,0:T(8,128)} %fusion.38), kind=kCustom, calls=%fused_computation.1.clone.1 | custom fusion | flops 2097152 | bytes 25166080 | tf_op jit(solution)/shard_map/while/body/eval_jaxpr/scatter-add | solution.py:28
  130.8 0.1 compare_and_fusion.2
  130.9 2.8 gather_fusion
  133.6 7.4 %fusion.38 = f32[64,128,256]{2,1,0:T(8,128)} fusion(bf16[64,128,256]{2,1,0:T(8,128)(2,1)} %gather_fusion, pred[64]{0:T(512)(128)(4,1)S(1)} %get-tuple-element.176, bf16[256,128,128]{2,1,0:T(8,128)(2,1)} %get-tuple-element.200, s32[]{:T(128)S(6)} %select_n.59), kind=kOutput, calls=%fused_computation.2.clone.1 | convolution fusion | flops 538968064 | bytes 14680132 | tf_op jit(solution)/shard_map/while/body/eval_jaxpr/gab,gbs->gas/dot_general | solution.py:27
  141.0 0.1 compare_select_fusion.4
  141.1 19.2 %scatter_fusion = f32[32,128,256]{2,1,0:T(8,128)} fusion(f32[32,128,256]{2,1,0:T(8,128)} %get-tuple-element.188, s32[64]{0:T(128)S(1)} %compare_select_fusion.4, f32[64,128,256]{2,1,0:T(8,128)} %fusion.38), kind=kCustom, calls=%fused_computation.1.clone.1 | custom fusion | flops 2097152 | bytes 25166080 | tf_op jit(solution)/shard_map/while/body/eval_jaxpr/scatter-add | solution.py:28
  160.3 0.0 reduce-scatter.2.cloned.1.call-update
  160.3 0.0 all-reduce.5.cloned.1.call-start
  160.3 50.9 %reduce-scatter.2.cloned.1.call-done = f32[512,256]{1,0:T(8,128)} async-done(((f32[4096,256]{1,0:T(8,128)}), f32[512,256]{1,0:T(8,128)}) %reduce-scatter.2.cloned.1.call-update) | async-done | bytes 524304 | tf_op jit(solution)/shard_map/reduce_scatter | solution.py:48
  211.2 2.2 fusion.11
  213.5 0.0 all-reduce.5.cloned.1.call-update
  213.5 0.0 all-reduce.7.cloned.1.call-start
  213.6 124.1 %all-reduce.5.cloned.1.call-done = f32[128,128]{0,1:T(8,128)} async-done(((f32[128,128]{0,1:T(8,128)}), f32[128,128]{0,1:T(8,128)}) %all-reduce.5.cloned.1.call-update) | async-done | bytes 65552 | tf_op jit(solution)/shard_map/psum | solution.py:53
  337.7 0.8 broadcast_multiply_fusion.2
  338.5 0.1 copy.7
  338.6 0.9 fusion.20
  339.5 11.7 %cholesky.44 = f32[128,128]{1,0:T(8,128)S(1)} custom-call(f32[128,128]{1,0:T(8,128)S(1)} %fusion.20), custom_call_target="Cholesky" | custom-call | tf_op jit(solution)/shard_map/jit(cholesky)/cholesky | solution.py:11
  351.2 0.6 compare_reduce_fusion.1
  351.8 0.7 fusion.22
  352.5 9.8 %custom-call.6 = f32[1,128,128]{1,2,0:T(8,128)S(1)} custom-call(f32[1,128,128]{2,1,0:T(8,128)S(1)} %get-tuple-element.131), custom_call_target="InvertDiagBlocksLowerTriangular" | custom-call | tf_op jit(solution)/shard_map/triangular_solve/custom-call.0 | solution.py:13
  362.3 0.3 fusion.15
  362.6 1.3 fusion.9
  364.0 2.2 fusion.7
  366.1 0.0 all-reduce.7.cloned.1.call-update
  366.2 0.2 all-reduce.9.cloned.1.call-start
  366.4 118.3 %all-reduce.7.cloned.1.call-done = f32[128,128]{0,1:T(8,128)} async-done(((f32[128,128]{0,1:T(8,128)}), f32[128,128]{0,1:T(8,128)}) %all-reduce.7.cloned.1.call-update) | async-done | bytes 65552 | tf_op jit(solution)/shard_map/psum | solution.py:58
  484.7 1.6 convolution_subtract_fusion
  486.3 1.2 fusion.24
  487.5 0.0 all-reduce.9.cloned.1.call-update
  487.5 0.8 broadcast_multiply_fusion.1
  488.3 121.6 %all-reduce.9.cloned.1.call-done = f32[128,128]{0,1:T(8,128)} async-done(((f32[128,128]{0,1:T(8,128)}), f32[128,128]{0,1:T(8,128)}) %all-reduce.9.cloned.1.call-update) | async-done | bytes 65552 | tf_op jit(solution)/shard_map/psum | solution.py:62
  610.0 0.8 broadcast_multiply_fusion
  610.8 0.1 copy.10
  610.9 0.9 fusion.18
  611.8 11.7 %cholesky.55 = f32[128,128]{1,0:T(8,128)S(1)} custom-call(f32[128,128]{1,0:T(8,128)S(1)} %fusion.18), custom_call_target="Cholesky" | custom-call | tf_op jit(solution)/shard_map/jit(cholesky)/cholesky | solution.py:11
  623.5 0.6 compare_reduce_fusion
  624.2 0.7 fusion.23
  624.8 0.8 copy.12
  625.7 9.8 %custom-call.7 = f32[1,128,128]{1,2,0:T(8,128)S(1)} custom-call(f32[1,128,128]{2,1,0:T(8,128)S(1)} %get-tuple-element.133), custom_call_target="InvertDiagBlocksLowerTriangular" | custom-call | tf_op jit(solution)/shard_map/triangular_solve/custom-call.0 | solution.py:13
  635.5 0.3 fusion.13
  635.8 0.4 fusion.25
  636.2 1.0 copy.11
  (9 shorter events, 0.2 us)
Async XLA Ops:
  7.2 32.3 %all-gather.2.cloned.1.call-start = ((), (), s32[]{:S(2)}) async-start(), calls=%async_computation.1 | async-start | bytes 1310720 | tf_op jit(solution)/shard_map/all_gather | solution.py:45
  7.9 203.3 %reduce-scatter.2.cloned.1.call-start = ((), (), s32[]{:S(2)}) async-start(), calls=%async_computation.2 | async-start | bytes 4718592 | tf_op jit(solution)/shard_map/reduce_scatter | solution.py:48
  39.5 2.5 copy-start
  160.3 177.4 %all-reduce.5.cloned.1.call-start = ((), (), s32[]{:S(2)}) async-start(), calls=%async_computation.3 | async-start | bytes 131072 | tf_op jit(solution)/shard_map/psum | solution.py:53
  213.5 271.2 %all-reduce.7.cloned.1.call-start = ((), (), s32[]{:S(2)}) async-start(), calls=%async_computation.4 | async-start | bytes 131072 | tf_op jit(solution)/shard_map/psum | solution.py:58
  366.2 243.8 %all-reduce.9.cloned.1.call-start = ((), (), s32[]{:S(2)}) async-start(), calls=%async_computation.5 | async-start | bytes 131072 | tf_op jit(solution)/shard_map/psum | solution.py:62
Sparse Core Ops, SparseCore 0:
  9.6 29.8 all-gather.1
  160.4 50.7 reduce-scatter.1
  218.3 119.2 all-reduce.4
  366.3 118.3 all-reduce.6
  491.6 118.3 all-reduce.8
where the time goes:
time: 644 us
  waiting for transfers between devices  446 us (69%)
  other arithmetic  128 us (20%)
  matrix products  39 us (6%)
  local copies, waits for them, and re-layouts  15.6 us (2%)
  between operations  13.9 us (2%)
    psum x1, waiting for transfers between devices, on_device(): lax.psum(jnp.dot(first_part.T, first_part, precision=high), ('row', 'col'))  124 us
    psum x1, waiting for transfers between devices, on_device(): lax.psum(jnp.dot(remainder.T, remainder, precision=high), ('row', 'col'))  122 us
    psum x1, waiting for transfers between devices, on_device(): lax.psum(jnp.dot(basis_one.T, second_part, precision=high), ('row', 'col'))  118 us
    scatter-add x4, other arithmetic, advance(): return summed.at[row_ids].add(product)  77.1 us
    reduce_scatter x1, waiting for transfers between devices, on_device(): lax.psum_scatter(partial_value, 'col', scatter_dimension=0, tiled=True)  50.9 us
    all_gather x1, waiting for transfers between devices, on_device(): gathered = lax.all_gather(gaussian_sketch, 'row', axis=0, tiled=True)  30.8 us
    dot_general x4, matrix products, advance(): jnp.einsum('gab,gbs->gas', values, picked, preferred_element_type=jnp.flo...  29.5 us
    another operation x6, other arithmetic, upper_parts(): lower_factor = jnp.linalg.cholesky(gram)  24.8 us
  transfers between devices with their start and end apart: 5, of which 5 were waited for; matrix products, arithmetic and copies ran while one was open for 0% of the time, Pallas kernels for 0%

commit v1 on v0

--- a/solution.py
+++ b/solution.py
@@ -50,7 +50,8 @@
     second_part = sketched[:, PANEL:]
     order_total = shard_rows * size_row * size_col
     gram_one = (
-        lax.psum(jnp.dot(first_part.T, first_part, precision=high), ("row", "col")) / order_total
+        lax.psum(lax.psum(jnp.dot(first_part.T, first_part, precision=high), "col"), "row")
+        / order_total
     )
     upper_one, inverse_one = upper_parts(gram_one)
     basis_one = jnp.dot(first_part, inverse_one, precision=high)

time: 644 us -> 611 us (0.949)
  waiting for transfers between devices: 446 us -> 413 us
    psum x1 -> x2, waiting for transfers between devices: 124 us -> 87.6 us  [the longest x1 53.4 us: on_device(): lax.psum(jnp.dot(first_part.T, first_part, precision=high), 'col')]
  transfers between devices with their start and end apart: 5 -> 6, of which waited for: 5 -> 6; matrix products, arithmetic and copies ran while one was open for 0% -> 0% of each run, Pallas kernels for 0% -> 0%
where the time goes in v1:
time: 611 us; the launch traced here: 610 us
  waiting for transfers between devices  413 us (68%)
  other arithmetic  128 us (21%)
  matrix products  39 us (6%)
  local copies, waits for them, and re-layouts  15.6 us (3%)
  between operations  14.2 us (2%)
    psum x1, waiting for transfers between devices, on_device(): lax.psum(jnp.dot(remainder.T, remainder, precision=high), ('row', 'col'))  122 us
    psum x1, waiting for transfers between devices, on_device(): lax.psum(jnp.dot(basis_one.T, second_part, precision=high), ('row', 'col'))  121 us
    scatter-add x4, other arithmetic, advance(): return summed.at[row_ids].add(product)  77.1 us
    psum x1, waiting for transfers between devices, on_device(): lax.psum(jnp.dot(first_part.T, first_part, precision=high), 'col')  53.4 us
    reduce_scatter x1, waiting for transfers between devices, on_device(): lax.psum_scatter(partial_value, 'col', scatter_dimension=0, tiled=True)  50.9 us
    psum x1, waiting for transfers between devices, on_device(): lax.psum(lax.psum(jnp.dot(first_part.T, first_part, precision=high), 'col...  34.2 us
    all_gather x1, waiting for transfers between devices, on_device(): gathered = lax.all_gather(gaussian_sketch, 'row', axis=0, tiled=True)  30.8 us
    dot_general x4, matrix products, advance(): jnp.einsum('gab,gbs->gas', values, picked, preferred_element_type=jnp.flo...  29.5 us
  transfers between devices with their start and end apart: 6, of which 6 were waited for; matrix products, arithmetic and copies ran while one was open for 0% of the time, Pallas kernels for 0%

profile of v1, /device:TPU:1, one launch (start us, length us, event | category | flops | bytes accessed | tf_op | source)
XLA Modules:
  0.0 610.3 jit_solution(32088975091075820)
XLA Ops:
  7.2 0.0 all-gather.2.cloned.1.call-start
  7.2 0.7 all-gather.2.cloned.1.call-update
  7.9 0.0 reduce-scatter.2.cloned.1.call-start
  8.0 0.7 broadcast_subtract_fusion
  8.7 30.8 %all-gather.2.cloned.1.call-done = bf16[2048,256]{1,0:T(8,128)(2,1)} async-done(((bf16[512,256]{1,0:T(8,128)(2,1)}), bf16[2048,256]{1,0:T(8,128)(2,1)}) %all-gather.2.cloned.1.call-update) | async-done | bytes 1048592 | tf_op jit(solution)/shard_map/all_gather | solution.py:45
  39.5 2.5 broadcast_in_dim.36
  41.9 118.3 %while.13 = (s32[]{:T(128)}, f32[32,128,256]{2,1,0:T(8,128)}, s32[256]{0:T(256)S(1)}, bf16[256,128,128]{2,1,0:T(8,128)(2,1)}, s32[256]{0:T(256)S(1)}, /*index=5*...) while((s32[]{:T(128)}, f32[32,128,256]{2,1,0:T(8,128)}, s32[256]{0:T(256)S(1)}, ...), condition=%wide.region_2.3_spmd, body=%wide.region_0.2_spmd.sunk | while | flops 541066816 | bytes 48240672 | solution.py:31
  41.9 0.1 compare_and_fusion.2
  42.0 2.8 gather_fusion
  44.8 7.4 %fusion.38 = f32[64,128,256]{2,1,0:T(8,128)} fusion(bf16[64,128,256]{2,1,0:T(8,128)(2,1)} %gather_fusion, pred[64]{0:T(512)(128)(4,1)S(1)} %get-tuple-element.176, bf16[256,128,128]{2,1,0:T(8,128)(2,1)} %get-tuple-element.200, s32[]{:T(128)S(6)} %select_n.59), kind=kOutput, calls=%fused_computation.2.clone.1 | convolution fusion | flops 538968064 | bytes 14680132 | tf_op jit(solution)/shard_map/while/body/eval_jaxpr/gab,gbs->gas/dot_general | solution.py:27
  52.2 0.1 compare_select_fusion.4
  52.3 19.2 %scatter_fusion = f32[32,128,256]{2,1,0:T(8,128)} fusion(f32[32,128,256]{2,1,0:T(8,128)} %get-tuple-element.188, s32[64]{0:T(128)S(1)} %compare_select_fusion.4, f32[64,128,256]{2,1,0:T(8,128)} %fusion.38), kind=kCustom, calls=%fused_computation.1.clone.1 | custom fusion | flops 2097152 | bytes 25166080 | tf_op jit(solution)/shard_map/while/body/eval_jaxpr/scatter-add | solution.py:28
  71.4 0.1 compare_and_fusion.2
  71.5 2.8 gather_fusion
  74.3 7.4 %fusion.38 = f32[64,128,256]{2,1,0:T(8,128)} fusion(bf16[64,128,256]{2,1,0:T(8,128)(2,1)} %gather_fusion, pred[64]{0:T(512)(128)(4,1)S(1)} %get-tuple-element.176, bf16[256,128,128]{2,1,0:T(8,128)(2,1)} %get-tuple-element.200, s32[]{:T(128)S(6)} %select_n.59), kind=kOutput, calls=%fused_computation.2.clone.1 | convolution fusion | flops 538968064 | bytes 14680132 | tf_op jit(solution)/shard_map/while/body/eval_jaxpr/gab,gbs->gas/dot_general | solution.py:27
  81.7 0.1 compare_select_fusion.4
  81.7 19.1 %scatter_fusion = f32[32,128,256]{2,1,0:T(8,128)} fusion(f32[32,128,256]{2,1,0:T(8,128)} %get-tuple-element.188, s32[64]{0:T(128)S(1)} %compare_select_fusion.4, f32[64,128,256]{2,1,0:T(8,128)} %fusion.38), kind=kCustom, calls=%fused_computation.1.clone.1 | custom fusion | flops 2097152 | bytes 25166080 | tf_op jit(solution)/shard_map/while/body/eval_jaxpr/scatter-add | solution.py:28
  100.9 0.1 compare_and_fusion.2
  101.0 2.8 gather_fusion
  103.7 7.4 %fusion.38 = f32[64,128,256]{2,1,0:T(8,128)} fusion(bf16[64,128,256]{2,1,0:T(8,128)(2,1)} %gather_fusion, pred[64]{0:T(512)(128)(4,1)S(1)} %get-tuple-element.176, bf16[256,128,128]{2,1,0:T(8,128)(2,1)} %get-tuple-element.200, s32[]{:T(128)S(6)} %select_n.59), kind=kOutput, calls=%fused_computation.2.clone.1 | convolution fusion | flops 538968064 | bytes 14680132 | tf_op jit(solution)/shard_map/while/body/eval_jaxpr/gab,gbs->gas/dot_general | solution.py:27
  111.1 0.1 compare_select_fusion.4
  111.2 19.6 %scatter_fusion = f32[32,128,256]{2,1,0:T(8,128)} fusion(f32[32,128,256]{2,1,0:T(8,128)} %get-tuple-element.188, s32[64]{0:T(128)S(1)} %compare_select_fusion.4, f32[64,128,256]{2,1,0:T(8,128)} %fusion.38), kind=kCustom, calls=%fused_computation.1.clone.1 | custom fusion | flops 2097152 | bytes 25166080 | tf_op jit(solution)/shard_map/while/body/eval_jaxpr/scatter-add | solution.py:28
  130.8 0.1 compare_and_fusion.2
  130.9 2.8 gather_fusion
  133.6 7.4 %fusion.38 = f32[64,128,256]{2,1,0:T(8,128)} fusion(bf16[64,128,256]{2,1,0:T(8,128)(2,1)} %gather_fusion, pred[64]{0:T(512)(128)(4,1)S(1)} %get-tuple-element.176, bf16[256,128,128]{2,1,0:T(8,128)(2,1)} %get-tuple-element.200, s32[]{:T(128)S(6)} %select_n.59), kind=kOutput, calls=%fused_computation.2.clone.1 | convolution fusion | flops 538968064 | bytes 14680132 | tf_op jit(solution)/shard_map/while/body/eval_jaxpr/gab,gbs->gas/dot_general | solution.py:27
  141.0 0.1 compare_select_fusion.4
  141.1 19.2 %scatter_fusion = f32[32,128,256]{2,1,0:T(8,128)} fusion(f32[32,128,256]{2,1,0:T(8,128)} %get-tuple-element.188, s32[64]{0:T(128)S(1)} %compare_select_fusion.4, f32[64,128,256]{2,1,0:T(8,128)} %fusion.38), kind=kCustom, calls=%fused_computation.1.clone.1 | custom fusion | flops 2097152 | bytes 25166080 | tf_op jit(solution)/shard_map/while/body/eval_jaxpr/scatter-add | solution.py:28
  160.3 0.0 reduce-scatter.2.cloned.1.call-update
  160.3 0.0 all-reduce.6.cloned.1.call-start
  160.3 50.9 %reduce-scatter.2.cloned.1.call-done = f32[512,256]{1,0:T(8,128)} async-done(((f32[4096,256]{1,0:T(8,128)}), f32[512,256]{1,0:T(8,128)}) %reduce-scatter.2.cloned.1.call-update) | async-done | bytes 524304 | tf_op jit(solution)/shard_map/reduce_scatter | solution.py:48
  211.2 2.2 fusion.11
  213.5 0.0 all-reduce.6.cloned.1.call-update
  213.5 0.0 all-reduce.8.cloned.1.call-start
  213.6 53.4 %all-reduce.6.cloned.1.call-done = f32[128,128]{0,1:T(8,128)} async-done(((f32[128,128]{0,1:T(8,128)}), f32[128,128]{0,1:T(8,128)}) %all-reduce.6.cloned.1.call-update) | async-done | bytes 65552 | tf_op jit(solution)/shard_map/psum | solution.py:53
  267.0 0.0 all-reduce.8.cloned.1.call-update
  267.0 0.0 all-reduce.10.cloned.1.call-start
  267.0 34.2 %all-reduce.8.cloned.1.call-done = f32[128,128]{0,1:T(8,128)} async-done(((f32[128,128]{0,1:T(8,128)}), f32[128,128]{0,1:T(8,128)}) %all-reduce.8.cloned.1.call-update) | async-done | bytes 65552 | tf_op jit(solution)/shard_map/psum | solution.py:53
  301.3 0.8 broadcast_multiply_fusion.2
  302.1 0.1 copy.7
  302.2 0.9 fusion.20
  303.1 11.7 %cholesky.44 = f32[128,128]{1,0:T(8,128)S(1)} custom-call(f32[128,128]{1,0:T(8,128)S(1)} %fusion.20), custom_call_target="Cholesky" | custom-call | tf_op jit(solution)/shard_map/jit(cholesky)/cholesky | solution.py:11
  314.8 0.6 compare_reduce_fusion.1
  315.5 0.7 fusion.22
  316.1 9.8 %custom-call.6 = f32[1,128,128]{1,2,0:T(8,128)S(1)} custom-call(f32[1,128,128]{2,1,0:T(8,128)S(1)} %get-tuple-element.131), custom_call_target="InvertDiagBlocksLowerTriangular" | custom-call | tf_op jit(solution)/shard_map/triangular_solve/custom-call.0 | solution.py:13
  325.9 0.3 fusion.15
  326.2 1.3 fusion.9
  327.6 2.2 fusion.7
  329.8 0.2 all-reduce.12.cloned.1.call-start
  330.0 120.9 %all-reduce.10.cloned.1.call-done = f32[128,128]{0,1:T(8,128)} async-done(((f32[128,128]{0,1:T(8,128)}), f32[128,128]{0,1:T(8,128)}) %all-reduce.10.cloned.1.call-update) | async-done | bytes 65552 | tf_op jit(solution)/shard_map/psum | solution.py:59
  450.9 1.6 convolution_subtract_fusion
  452.5 1.2 fusion.24
  453.7 0.8 broadcast_multiply_fusion.1
  454.6 121.6 %all-reduce.12.cloned.1.call-done = f32[128,128]{0,1:T(8,128)} async-done(((f32[128,128]{0,1:T(8,128)}), f32[128,128]{0,1:T(8,128)}) %all-reduce.12.cloned.1.call-update) | async-done | bytes 65552 | tf_op jit(solution)/shard_map/psum | solution.py:63
  576.2 0.8 broadcast_multiply_fusion
  577.0 0.1 copy.10
  577.1 0.9 fusion.18
  578.0 11.7 %cholesky.55 = f32[128,128]{1,0:T(8,128)S(1)} custom-call(f32[128,128]{1,0:T(8,128)S(1)} %fusion.18), custom_call_target="Cholesky" | custom-call | tf_op jit(solution)/shard_map/jit(cholesky)/cholesky | solution.py:11
  589.7 0.6 compare_reduce_fusion
  590.4 0.7 fusion.23
  591.1 0.8 copy.12
  591.9 9.8 %custom-call.7 = f32[1,128,128]{1,2,0:T(8,128)S(1)} custom-call(f32[1,128,128]{2,1,0:T(8,128)S(1)} %get-tuple-element.133), custom_call_target="InvertDiagBlocksLowerTriangular" | custom-call | tf_op jit(solution)/shard_map/triangular_solve/custom-call.0 | solution.py:13
  601.7 0.3 fusion.13
  602.0 0.4 fusion.25
  602.5 1.0 copy.11
  (12 shorter events, 0.2 us)
Async XLA Ops:
  7.2 32.3 %all-gather.2.cloned.1.call-start = ((), (), s32[]{:S(2)}) async-start(), calls=%async_computation.1 | async-start | bytes 1310720 | tf_op jit(solution)/shard_map/all_gather | solution.py:45
  7.9 203.3 %reduce-scatter.2.cloned.1.call-start = ((), (), s32[]{:S(2)}) async-start(), calls=%async_computation.2 | async-start | bytes 4718592 | tf_op jit(solution)/shard_map/reduce_scatter | solution.py:48
  39.5 2.5 copy-start
  160.3 106.7 %all-reduce.6.cloned.1.call-start = ((), (), s32[]{:S(2)}) async-start(), calls=%async_computation.3 | async-start | bytes 131072 | tf_op jit(solution)/shard_map/psum | solution.py:53
  213.5 87.8 %all-reduce.8.cloned.1.call-start = ((), (), s32[]{:S(2)}) async-start(), calls=%async_computation.4 | async-start | bytes 131072 | tf_op jit(solution)/shard_map/psum | solution.py:53
  267.0 183.9 %all-reduce.10.cloned.1.call-start = ((), (), s32[]{:S(2)}) async-start(), calls=%async_computation.5 | async-start | bytes 131072 | tf_op jit(solution)/shard_map/psum | solution.py:59
  329.8 246.4 %all-reduce.12.cloned.1.call-start = ((), (), s32[]{:S(2)}) async-start(), calls=%async_computation.6 | async-start | bytes 131072 | tf_op jit(solution)/shard_map/psum | solution.py:63
Sparse Core Ops, SparseCore 0:
  9.6 29.8 all-gather.1
  160.4 50.7 reduce-scatter.1
  215.2 51.7 all-reduce.5
  269.1 32.0 all-reduce.7
  329.9 120.9 all-reduce.9
  457.8 118.3 all-reduce.11
